TPU v7x, 512 devices: a whole 4x4x16 slice. The times are simulated.
512 devices in a mesh: subtree: 16 (over z), forest: 32 (over y, x, core).
Axes of the slice: x: 4, y: 4, z: 16, core: 2. Of those that a mesh axis runs over, the one named last changes fastest.
Arguments:
- panels: bfloat16 [16, 32, 1024, 2048], P('subtree', 'forest'), may hold values from -0.75 to 0.75
- pattern: int32 [16, 32, 8, 8], P('subtree', 'forest'), may hold values from 0 to 1, as said below
- child_map: int32 [16, 32, 8], P('subtree', 'forest'), may hold values from 0 to 7, each once within a row
- ancestor_map: int32 [16, 32, 8], P('subtree', 'forest'), may hold values from 0 to 95, as said below
Outputs:
- ancestors: float32 [16, 96, 64, 128], P('subtree', 'forest')
Inputs may be any that keep to these rules, and one draw needn't show every extreme that they name: pattern[s, f, i, j] = pattern[s, f, i, i] * pattern[s, f, j, j], so each pattern is symmetric; every panel has at least one occupied and at least one empty block row. No two entries of ancestor_map[s, f, :] have the same value of entry // 3.
All inputs are finite; a program needn't handle non-finite values.
Results may differ from a plain program's by a relative error of at most 0.0003.
Values sent between devices are 32-bit elements; how exact they have to be, the bound alone decides.
A program may use at most 64 MiB of HBM per device.

v0:
```python
import jax
import jax.numpy as jnp
from jax import lax
from jax.sharding import PartitionSpec as P

ANC_DEV = 3


def swapped(shard, axis, apart):
    return lax.ppermute(shard, axis, [(i, i ^ 1 << apart) for i in range(lax.axis_size(axis))])


def per_device(panels, pattern, child_map, ancestor_map):
    row_total = panels.shape[2]
    pivot_width = panels.shape[3]
    block_count = child_map.shape[2]
    block_rows = row_total // block_count
    blocks = panels[0, 0].reshape(block_count, block_rows, pivot_width)
    one_hot = child_map[0, 0][:, None] == jnp.arange(block_count, dtype=jnp.int32)[None, :]
    reordered = jnp.einsum(
        "im,ipk->mpk", one_hot.astype(jnp.bfloat16), blocks, preferred_element_type=jnp.float32
    ).astype(jnp.bfloat16)
    flat_rows = reordered.reshape(row_total, pivot_width)
    hot_float = one_hot.astype(jnp.float32)
    moved_pattern = jnp.dot(
        jnp.dot(hot_float.T, pattern[0, 0].astype(jnp.float32), precision=lax.Precision.HIGHEST),
        hot_float,
        precision=lax.Precision.HIGHEST,
    )
    update = lax.dot_general(
        flat_rows, flat_rows, (((1,), (1,)), ((), ())), preferred_element_type=jnp.float32
    )
    update = (
        update.reshape(block_count, block_rows, block_count, block_rows)
        * moved_pattern[:, None, :, None]
    ).reshape(row_total, row_total)
    sub_count = lax.axis_size("subtree")
    depth = sub_count.bit_length() - 1
    my_index = lax.axis_index("subtree")
    holding = update
    for depth_step in range(depth):
        bit_number = depth - 1 - depth_step
        half_rows = holding.shape[0] // 2
        low_half = holding[:half_rows]
        high_half = holding[half_rows:]
        high_side = my_index >> bit_number & 1 == 1
        kept_half = jnp.where(high_side, high_half, low_half)
        sent_half = jnp.where(high_side, low_half, high_half)
        holding = kept_half + swapped(sent_half, "subtree", bit_number)
    piece_rows = holding.shape[0]
    column_blocks = holding.reshape(piece_rows, block_count, block_rows).transpose(1, 0, 2)
    slot_values = ancestor_map[0, 0]
    tree_count = lax.axis_size("forest")
    slot_total = ANC_DEV * tree_count
    slot_hot = (slot_values[:, None] == jnp.arange(slot_total, dtype=jnp.int32)[None, :]).astype(
        jnp.float32
    )
    slot_terms = jnp.einsum("ca,cpq->apq", slot_hot, column_blocks, precision=lax.Precision.HIGHEST)
    summed = lax.psum_scatter(slot_terms, "forest", scatter_dimension=0, tiled=True)
    return summed[None]


def solution(mesh):
    in_specs = (
        P("subtree", "forest", None, None),
        P("subtree", "forest", None, None),
        P("subtree", "forest", None),
        P("subtree", "forest", None),
    )
    out_specs = P("subtree", "forest", None, None)
    return jax.shard_map(
        per_device, mesh=mesh, in_specs=in_specs, out_specs=out_specs, check_vma=False
    )
```

profile of v0, /device:TPU:1, one launch (start us, length us, event | category | flops | bytes accessed | tf_op | source)
XLA Modules:
  0.0 476.0 jit_solution(12273118531128815414)
XLA Ops:
  6.5 0.0 reduce-scatter.2.cloned.1.call-start
  6.5 0.8 fusion.16
  7.4 0.8 fusion.19
  8.1 7.0 %fusion.6 = bf16[8,128,2048]{2,0,1:T(8,128)(2,1)} fusion(bf16[8,128,2048]{2,1,0:T(8,128)(2,1)} %bitcast.37, s32[8]{0:T(128)} %bitcast.42), kind=kOutput, calls=%fused_computation.6 | convolution fusion | flops 35651648 | bytes 8388640 | tf_op jit(solution)/shard_map/im,ipk->mpk/dot_general | solution.py:20
  15.2 19.9 %fusion.9 = f32[8,128,8,128]{3,1,2,0:T(8,128)S(1)} fusion(bf16[8,128,2048]{2,0,1:T(8,128)(2,1)} %fusion.6, bf16[8,128,2048,1]{2,0,1,3:T(8,128)(2,1)} %bitcast.38, f32[8,8]{1,0:T(8,128)S(1)} %fusion.19), kind=kOutput, calls=%fused_computation.7 | convolution fusion | flops 4296015872 | bytes 12583168 | tf_op jit(solution)/shard_map/dot_general | solution.py:30
  35.1 0.3 slice_select_fusion.1
  35.4 1.2 copy.13
  36.7 1.8 copy.37
  38.4 16.5 %collective-permute-start = (f32[512,1024]{1,0:T(8,128)}, f32[512,1024]{1,0:T(8,128)S(1)}, u32[]{:S(2)}, u32[]{:S(2)}) collective-permute-start(f32[512,1024]{1,0:T(8,128)} %bitcast.34), channel_id=1, source_target_pairs={{0,256},{32,288},{64,320},{96,352},{128,384},{160,416},{192,448},{... | collective-permute-start | bytes 6291464 | tf_op jit(solution)/shard_map/ppermute | solution.py:10
  54.9 2.6 copy.12
  57.5 76.4 %collective-permute-done = f32[512,1024]{1,0:T(8,128)S(1)} collective-permute-done((f32[512,1024]{1,0:T(8,128)}, f32[512,1024]{1,0:T(8,128)S(1)}, u32[]{:S(2)}, u32[]{:S(2)}) %collective-permute-start) | collective-permute-done | bytes 2097184 | tf_op jit(solution)/shard_map/ppermute | solution.py:10
  133.9 0.0 copy-start
  133.9 1.3 copy-done
  135.2 2.9 bitcast_add_fusion
  138.2 0.2 slice_select_fusion.2
  138.4 87.7 %collective-permute-start.1 = (f32[256,1024]{1,0:T(8,128)S(1)}, f32[256,1024]{1,0:T(8,128)}, u32[]{:S(2)}, u32[]{:S(2)}) collective-permute-start(f32[256,1024]{1,0:T(8,128)S(1)} %slice_select_fusion.2), channel_id=1, source_target_pairs={{0,128},{32,160},{64,192},{96,224},{128,0},{160,32},{192,64},{224,... | collective-permute-start | bytes 3145736 | tf_op jit(solution)/shard_map/ppermute | solution.py:10
  226.1 0.0 copy-start.1
  226.1 100.7 %collective-permute-done.1 = f32[256,1024]{1,0:T(8,128)} collective-permute-done((f32[256,1024]{1,0:T(8,128)S(1)}, f32[256,1024]{1,0:T(8,128)}, u32[]{:S(2)}, u32[]{:S(2)}) %collective-permute-start.1) | collective-permute-done | bytes 1048608 | tf_op jit(solution)/shard_map/ppermute | solution.py:10
  326.8 1.5 select_add_fusion
  328.3 0.1 slice_select_fusion.3
  328.4 1.9 collective-permute-start.2
  330.3 23.7 %collective-permute-done.2 = f32[128,1024]{1,0:T(8,128)S(1)} collective-permute-done((f32[128,1024]{1,0:T(8,128)S(1)}, f32[128,1024]{1,0:T(8,128)S(1)}, u32[]{:S(2)}, u32[]{:S(2)}) %collective-permute-start.2) | collective-permute-done | bytes 524320 | tf_op jit(solution)/shard_map/ppermute | solution.py:10
  354.0 0.1 select_add_fusion.1
  354.2 1.9 collective-permute-start.3
  356.1 7.3 %collective-permute-done.3 = f32[64,1024]{1,0:T(8,128)S(1)} collective-permute-done((f32[64,1024]{1,0:T(8,128)S(1)}, f32[64,1024]{1,0:T(8,128)S(1)}, u32[]{:S(2)}, u32[]{:S(2)}) %collective-permute-start.3) | collective-permute-done | bytes 262176 | tf_op jit(solution)/shard_map/ppermute | solution.py:10
  363.4 0.1 add_bitcast_fusion
  363.5 0.0 copy-done.1
  363.6 1.5 fusion.14
  365.1 3.5 copy.14
  368.5 0.0 reduce-scatter.2.cloned.1.call-update
  368.6 100.6 %reduce-scatter.2.cloned.1.call-done = f32[3,64,128]{2,1,0:T(8,128)} async-done(((f32[96,64,128]{2,1,0:T(8,128)}), f32[3,64,128]{2,1,0:T(8,128)}) %reduce-scatter.2.cloned.1.call-update) | async-done | bytes 98320 | tf_op jit(solution)/shard_map/reduce_scatter | solution.py:59
  (2 shorter events, 0.1 us)
Async XLA Ops:
  6.5 462.6 %reduce-scatter.2.cloned.1.call-start = ((), (), s32[]{:S(2)}) async-start(), calls=%async_computation.1 | async-start | bytes 3244032 | tf_op jit(solution)/shard_map/reduce_scatter | solution.py:59
  38.4 95.5 %collective-permute-start = (f32[512,1024]{1,0:T(8,128)}, f32[512,1024]{1,0:T(8,128)S(1)}, u32[]{:S(2)}, u32[]{:S(2)}) collective-permute-start(f32[512,1024]{1,0:T(8,128)} %bitcast.34), channel_id=1, source_target_pairs={{0,256},{32,288},{64,320},{96,352},{128,384},{160,416},{192,448},{... | collective-permute-start | bytes 6291464 | tf_op jit(solution)/shard_map/ppermute | solution.py:10
  133.9 1.3 copy-start
  138.4 188.4 %collective-permute-start.1 = (f32[256,1024]{1,0:T(8,128)S(1)}, f32[256,1024]{1,0:T(8,128)}, u32[]{:S(2)}, u32[]{:S(2)}) collective-permute-start(f32[256,1024]{1,0:T(8,128)S(1)} %slice_select_fusion.2), channel_id=1, source_target_pairs={{0,128},{32,160},{64,192},{96,224},{128,0},{160,32},{192,64},{224,... | collective-permute-start | bytes 3145736 | tf_op jit(solution)/shard_map/ppermute | solution.py:10
  226.1 137.5 %copy-start.1 = (s32[1,1,8]{2,1,0:T(1,128)S(1)}, s32[1,1,8]{2,1,0:T(1,128)}, u32[]{:S(2)}) copy-start(s32[1,1,8]{2,1,0:T(1,128)} %param.7) | copy-start | bytes 100
  328.4 25.6 %collective-permute-start.2 = (f32[128,1024]{1,0:T(8,128)S(1)}, f32[128,1024]{1,0:T(8,128)S(1)}, u32[]{:S(2)}, u32[]{:S(2)}) collective-permute-start(f32[128,1024]{1,0:T(8,128)S(1)} %slice_select_fusion.3), channel_id=1, source_target_pairs={{0,64},{32,96},{64,0},{96,32},{128,192},{160,224},{192,128},{224,1... | collective-permute-start | bytes 1572872 | tf_op jit(solution)/shard_map/ppermute | solution.py:10
  354.2 9.3 %collective-permute-start.3 = (f32[64,1024]{1,0:T(8,128)S(1)}, f32[64,1024]{1,0:T(8,128)S(1)}, u32[]{:S(2)}, u32[]{:S(2)}) collective-permute-start(f32[64,1024]{1,0:T(8,128)S(1)} %slice_select_fusion.4), channel_id=1, source_target_pairs={{0,32},{32,0},{64,96},{96,64},{128,160},{160,128},{192,224},{224,1... | collective-permute-start | bytes 786440 | tf_op jit(solution)/shard_map/ppermute | solution.py:10
Sparse Core Ops, SparseCore 0:
  368.7 100.4 reduce-scatter.1
where the time goes:
time: 477 us; the launch traced here: 476 us
  waiting for transfers between devices  309 us (65%)
  starting transfers between devices  108 us (23%)
  matrix products  30.1 us (6%)
  between operations  13.5 us (3%)
  local copies, waits for them, and re-layouts  10.4 us (2%)
  other arithmetic  5.18 us (1%)
    ppermute x4, waiting for transfers between devices, swapped(): lax.ppermute(shard, axis, [(i, i ^ 1 << apart) for i in range(lax.axis_si...  208 us
    ppermute x4, starting transfers between devices, swapped(): lax.ppermute(shard, axis, [(i, i ^ 1 << apart) for i in range(lax.axis_si...  108 us
    reduce_scatter x1, waiting for transfers between devices, per_device(): lax.psum_scatter(slot_terms, 'forest', scatter_dimension=0, tiled=True)  101 us
    dot_general x1, matrix products, per_device(): lax.dot_general(flat_rows, flat_rows, (((1,), (1,)), ((), ())), preferred...  19.9 us
  transfers between devices with their start and end apart: 5, of which 5 were waited for; matrix products, arithmetic and copies ran while one was open for 1% of the time, Pallas kernels for 0%

commit v1 on v0

v1 whole, which is shorter than its diff:
```python
import jax
import jax.numpy as jnp
from jax import lax
from jax.experimental import pallas as pl
from jax.experimental.pallas import tpu as pltpu
from jax.sharding import PartitionSpec as P

MESH = pl.DeviceIdType.MESH
ANC_DEV = 3
OWNED = (5, 2, 1, 4, 0)
SENT = 3
LAG = (0, 0, 0, 0, 0)


def kernel(
    subs, trees,
    child_ref, pattern_ref, anc_ref, panel_ref, out_ref,
    rows, gram, recv_l, recv_s, piece, x_send, x_recv, w_send, w_recv, t_send, t_recv,
    l_out, l_in, s_out, s_in, x_out, x_in, w_out, w_in, t_out, t_in,
):
    nb = child_ref.shape[0]
    block = panel_ref.shape[1]
    part = block // 2
    half = subs // 2
    s = lax.axis_index("subtree")
    f = lax.axis_index("forest")
    m = s // 2
    side = s % 2
    sigma = 1 - 2 * (f % 2)

    def z(offset):
        return (s + offset + 4 * subs) % subs

    def block_row(offset):
        return (m + offset + 4 * nb) % nb

    barrier = pltpu.get_barrier_semaphore()
    others = [(z(0) // 2 * 2 + 1 - side, f)]
    for e in (1, 2, 3):
        for sign in (1, -1):
            for j in (0, 1):
                others.append((2 * block_row(sign * e) + j, f))
    for other in others:
        pl.semaphore_signal(barrier, inc=1, device_id=other, device_id_type=MESH)

    @pl.loop(1, trees)
    def _(r):
        pl.semaphore_signal(
            barrier, inc=1, device_id=(s, (f + r) % trees), device_id_type=MESH
        )

    @pl.loop(0, nb)
    def _(to):
        source = jnp.int32(0)
        for i in range(nb):
            source = jnp.where(child_ref[i] == to, i, source)
        keep = jnp.int32(0)
        for i in range(nb):
            keep = jnp.where(child_ref[i] == to, pattern_ref[i, i], keep)
        chunk = panel_ref[source]
        rows[pl.ds(pl.multiple_of(to * block, block), block), :] = chunk * keep.astype(
            jnp.float32
        ).astype(jnp.bfloat16)

    @pl.loop(0, nb // 2)
    def _(u):
        at = pl.ds(pl.multiple_of(u * 2 * block, 2 * block), 2 * block)
        product = lax.dot_general(
            rows[at, :], rows[...], (((1,), (1,)), ((), ())), preferred_element_type=jnp.float32
        )
        for n in range(nb):
            gram[n, at, :] = product[:, n * block : (n + 1) * block]

    pl.semaphore_wait(barrier, len(others) + trees - 1)

    row = lax.broadcasted_iota(jnp.int32, w_send.shape[1:], 0)

    def weights(owner):
        total = jnp.zeros(row.shape, jnp.float32)
        for c in range(nb):
            total += jnp.where(row == anc_ref[c] - ANC_DEV * owner, 1.0, 0.0)
        return total

    def w_copy(r, owner, source):
        return pltpu.make_async_remote_copy(
            src_ref=w_send.at[owner], dst_ref=w_recv.at[source],
            send_sem=w_out.at[r], recv_sem=w_in.at[r],
            device_id=(s, owner), device_id_type=MESH,
        )

    def t_copy(r, owner, source):
        return pltpu.make_async_remote_copy(
            src_ref=t_send.at[owner], dst_ref=t_recv.at[source],
            send_sem=t_out.at[r], recv_sem=t_in.at[r],
            device_id=(s, owner), device_id_type=MESH,
        )

    def own(target, j):
        return gram.at[
            block_row_of(target, j), pl.ds(pl.multiple_of(target * part, part), part), :
        ]

    def block_row_of(target, j):
        return (target // 2 + OWNED[j]) % nb

    def chain(k, j, buffers, outs, ins, direction, steps):
        target = z(direction * (steps - k))
        if k == 0:
            source = own(target, j)
        else:
            source = buffers.at[k - 1, j]
        return pltpu.make_async_remote_copy(
            src_ref=source, dst_ref=buffers.at[k, j],
            send_sem=outs.at[k, j], recv_sem=ins.at[k, j],
            device_id=(z(direction), f), device_id_type=MESH,
        )

    def advance(k, j, buffers, outs, ins, direction, steps):
        if k > 0:
            chain(k - 1, j, buffers, outs, ins, direction, steps).wait_recv()
            buffers[k - 1, j] = buffers[k - 1, j] + own(z(direction * (steps - k)), j)[...]
        chain(k, j, buffers, outs, ins, direction, steps).start()

    long_chain = (recv_l, l_out, l_in, sigma, half)
    short_chain = (recv_s, s_out, s_in, -sigma, half - 1)

    def x_copy(j, other):
        n = block_row(OWNED[j])
        return pltpu.make_async_remote_copy(
            src_ref=x_send.at[j, other], dst_ref=x_recv.at[j, side],
            send_sem=x_out.at[j, other], recv_sem=x_in.at[j, side],
            device_id=(2 * n + other, f), device_id_type=MESH,
        )

    def x_arrival(j, other):
        return pltpu.make_async_remote_copy(
            src_ref=x_send.at[j, other], dst_ref=x_recv.at[j, other],
            send_sem=x_out.at[j, other], recv_sem=x_in.at[j, other],
            device_id=(2 * block_row(OWNED[j]) + other, f), device_id_type=MESH,
        )

    quarter = part // 2

    def finish(j):
        chain(half - 1, j, *long_chain).wait_recv()
        chain(half - 2, j, *short_chain).wait_recv()
        tile = own(z(0), j)[...] + (recv_l[half - 1, j] + recv_s[half - 2, j])
        piece[block_row(OWNED[j])] = tile
        if j < SENT:
            stacked = jnp.concatenate([tile, pltpu.roll(tile, block - quarter, 1)], axis=0)
            turned = stacked.T
            for other in (0, 1):
                x_send[j, other] = turned[other * part : other * part + quarter, :]
                x_copy(j, other).start()

    order = sorted(
        (k + LAG[j], j, k) for k in range(half + 1) for j in range(len(OWNED))
    )
    started = False
    for _, j, k in order:
        if k < half:
            advance(k, j, *long_chain)
        if k < half - 1:
            advance(k, j, *short_chain)
        if k == half:
            finish(j)
        if k == 1 and not started:
            started = True
            w_send[f] = weights(f)
            w_recv[f] = weights(f)

            @pl.loop(1, trees)
            def _(r):
                owner = (f + r) % trees
                w_send[owner] = weights(owner)
                w_copy(r, owner, f).start()

    lane = lax.broadcasted_iota(jnp.int32, (quarter, block), 1)
    for j in range(SENT):
        for other in (0, 1):
            x_arrival(j, other).wait_recv()
        low = x_recv[j, 0]
        high = x_recv[j, 1]
        n = block_row(-OWNED[j])
        piece[n, :quarter, :] = jnp.where(lane < part, low, pltpu.roll(high, part, 1))
        piece[n, quarter:, :] = jnp.where(lane < part, pltpu.roll(low, part, 1), high)
    piece[nb] = jnp.zeros(piece.shape[1:], jnp.float32)

    def chosen(owner):
        index = jnp.int32(nb)
        for c in range(nb):
            first = anc_ref[c] - ANC_DEV * owner
            index = jnp.where((first >= 0) & (first < ANC_DEV), c, index)
        return piece[index]

    @pl.loop(1, trees)
    def _(r):
        owner = (f + r) % trees
        t_send[owner] = chosen(owner)
        t_copy(r, owner, f).start()

    def added(source, tile, totals):
        weight = w_recv[source]
        return tuple(totals[a] + weight[a : a + 1, :] * tile for a in range(ANC_DEV))

    zero = jnp.zeros(piece.shape[1:], jnp.float32)
    totals = added(f, chosen(f), (zero,) * ANC_DEV)

    def gather(r, totals):
        source = (f + trees - r) % trees
        w_copy(r, source, source).wait_recv()
        t_copy(r, source, source).wait_recv()
        return added(source, t_recv[source], totals)

    totals = lax.fori_loop(1, trees, gather, totals)
    for a in range(ANC_DEV):
        out_ref[a] = totals[a]

    for j in range(len(OWNED)):
        for k in range(half):
            chain(k, j, *long_chain).wait_send()
        for k in range(half - 1):
            chain(k, j, *short_chain).wait_send()
    for j in range(SENT):
        for other in (0, 1):
            x_copy(j, other).wait_send()

    @pl.loop(1, trees)
    def _(r):
        owner = (f + r) % trees
        w_copy(r, owner, f).wait_send()
        t_copy(r, owner, f).wait_send()


def solution(mesh):
    subs, trees = mesh.shape["subtree"], mesh.shape["forest"]

    def per_device(panels, pattern, child_map, ancestor_map):
        rows, depth = panels.shape[2:]
        nb = child_map.shape[2]
        block = rows // nb
        part = block // 2
        half = subs // 2
        owned = len(OWNED)
        dma = pltpu.SemaphoreType.DMA
        smem = pl.BlockSpec(memory_space=pltpu.SMEM)
        vmem = pl.BlockSpec(memory_space=pltpu.VMEM)
        f32 = jnp.float32
        out = pl.pallas_call(
            lambda *refs: kernel(subs, trees, *refs),
            name="assemble",
            out_shape=jax.ShapeDtypeStruct((ANC_DEV, part, block), f32),
            in_specs=[smem, smem, smem, vmem],
            out_specs=vmem,
            scratch_shapes=[
                pltpu.VMEM((rows, depth), jnp.bfloat16),
                pltpu.VMEM((nb, rows, block), f32),
                pltpu.VMEM((half, owned, part, block), f32),
                pltpu.VMEM((half - 1, owned, part, block), f32),
                pltpu.VMEM((nb + 1, part, block), f32),
                pltpu.VMEM((SENT, 2, part // 2, block), f32),
                pltpu.VMEM((SENT, 2, part // 2, block), f32),
                pltpu.VMEM((trees, 8, block), f32),
                pltpu.VMEM((trees, 8, block), f32),
                pltpu.VMEM((trees, part, block), f32),
                pltpu.VMEM((trees, part, block), f32),
                dma((half, owned)), dma((half, owned)),
                dma((half - 1, owned)), dma((half - 1, owned)),
                dma((SENT, 2)), dma((SENT, 2)),
                dma((trees,)), dma((trees,)),
                dma((trees,)), dma((trees,)),
            ],
            compiler_params=pltpu.CompilerParams(
                collective_id=0, has_side_effects=True, vmem_limit_bytes=60 * 2**20
            ),
        )(child_map[0, 0], pattern[0, 0], ancestor_map[0, 0], panels.reshape(nb, block, depth))
        return out[None]

    return jax.shard_map(
        per_device,
        mesh=mesh,
        in_specs=(
            P("subtree", "forest", None, None),
            P("subtree", "forest", None, None),
            P("subtree", "forest", None),
            P("subtree", "forest", None),
        ),
        out_specs=P("subtree", "forest", None, None),
        check_vma=False,
    )
```

time: 477 us -> 71.3 us (0.15)
  waiting for transfers between devices: 309 us -> 0 us
  starting transfers between devices: 108 us -> 0 us
  Pallas kernels: 0 us -> 69.6 us
  matrix products: 30.1 us -> 0 us
  between operations: 13.5 us -> 0.01 us
  local copies, waits for them, and re-layouts: 10.4 us -> 1.54 us
  other arithmetic: 5.18 us -> 0 us
    ppermute x4 -> x0, waiting for transfers between devices: 208 us -> none  [swapped(): lax.ppermute(shard, axis, [(i, i ^ 1 << apart) for i in range(lax.axis_si...]
    ppermute x4 -> x0, starting transfers between devices: 108 us -> none  [swapped(): lax.ppermute(shard, axis, [(i, i ^ 1 << apart) for i in range(lax.axis_si...]
    reduce_scatter x1 -> x0, waiting for transfers between devices: 101 us -> none  [per_device(): lax.psum_scatter(slot_terms, 'forest', scatter_dimension=0, tiled=True)]
    pallas_call x0 -> x1, Pallas kernels: none -> 69.6 us  [per_device(): pl.pallas_call(lambda *refs: kernel(subs, trees, *refs), name='assemble',...]
    dot_general x5 -> x0, matrix products: 30.1 us -> none  [the longest x1 19.9 us: per_device(): lax.dot_general(flat_rows, flat_rows, (((1,), (1,)), ((), ())), preferred...]
  transfers between devices with their start and end apart: 5 -> 0, of which waited for: 5 -> 0; matrix products, arithmetic and copies ran while one was open for 1% -> 0% of each run, Pallas kernels for 0% -> 0%
where the time goes in v1:
time: 71.3 us; the launch traced here: 71.1 us
  Pallas kernels  69.6 us (98%)
  local copies, waits for them, and re-layouts  1.54 us (2%)
    pallas_call x1, Pallas kernels, per_device(): pl.pallas_call(lambda *refs: kernel(subs, trees, *refs), name='assemble',...  69.6 us
    unnamed x1, local copies, waits for them, and re-layouts  1.54 us

profile of v1, /device:TPU:1, one launch (start us, length us, event | category | flops | bytes accessed | tf_op | source)
XLA Modules:
  0.0 71.1 jit_solution(6662342170985416322)
XLA Ops:
  0.0 69.6 %assemble.1 = f32[3,64,128]{2,1,0:T(8,128)} custom-call(s32[8]{0:T(128)} %bitcast.8, s32[8,8]{1,0:T(8,128)} %bitcast.7, s32[8]{0:T(128)} %bitcast.9, bf16[8,128,2048]{2,1,0:T(8,128)(2,1)} %bitcast.5), custom_call_target="tpu_custom_call" | custom-call | tf_op jit(solution)/shard_map/assemble/pallas_call | solution.py:249
  69.6 1.5 %copy.6 = f32[1,3,64,128]{3,2,1,0:T(8,128)} copy(f32[1,3,64,128]{3,2,1,0:T(8,128)} %bitcast.6) | data formatting | bytes 196608

commit v2 on v1

--- a/solution.py
+++ b/solution.py
@@ -14,12 +14,12 @@
 
 def kernel(
     subs, trees,
-    child_ref, pattern_ref, anc_ref, panel_ref, out_ref,
-    rows, gram, recv_l, recv_s, piece, x_send, x_recv, w_send, w_recv, t_send, t_recv,
-    l_out, l_in, s_out, s_in, x_out, x_in, w_out, w_in, t_out, t_in,
+    child_ref, pattern_ref, anc_ref, panel_hbm, out_ref,
+    panel_ref, rows, gram, recv_l, recv_s, piece, x_send, x_recv, w_send, w_recv, t_send, t_recv,
+    l_out, l_in, s_out, s_in, x_out, x_in, w_out, w_in, t_out, t_in, panel_in,
 ):
     nb = child_ref.shape[0]
-    block = panel_ref.shape[1]
+    block = panel_hbm.shape[1]
     part = block // 2
     half = subs // 2
     s = lax.axis_index("subtree")
@@ -34,20 +34,20 @@
     def block_row(offset):
         return (m + offset + 4 * nb) % nb
 
+    load = pltpu.make_async_copy(panel_hbm, panel_ref, panel_in)
+    load.start()
+
     barrier = pltpu.get_barrier_semaphore()
-    others = [(z(0) // 2 * 2 + 1 - side, f)]
-    for e in (1, 2, 3):
-        for sign in (1, -1):
-            for j in (0, 1):
-                others.append((2 * block_row(sign * e) + j, f))
-    for other in others:
-        pl.semaphore_signal(barrier, inc=1, device_id=other, device_id_type=MESH)
+    for step in (1, -1):
+        pl.semaphore_signal(barrier, inc=1, device_id=(z(step), f), device_id_type=MESH)
 
     @pl.loop(1, trees)
     def _(r):
         pl.semaphore_signal(
             barrier, inc=1, device_id=(s, (f + r) % trees), device_id_type=MESH
         )
+
+    load.wait()
 
     @pl.loop(0, nb)
     def _(to):
@@ -62,8 +62,7 @@
             jnp.float32
         ).astype(jnp.bfloat16)
 
-    @pl.loop(0, nb // 2)
-    def _(u):
+    def multiply(u):
         at = pl.ds(pl.multiple_of(u * 2 * block, 2 * block), 2 * block)
         product = lax.dot_general(
             rows[at, :], rows[...], (((1,), (1,)), ((), ())), preferred_element_type=jnp.float32
@@ -71,7 +70,10 @@
         for n in range(nb):
             gram[n, at, :] = product[:, n * block : (n + 1) * block]
 
-    pl.semaphore_wait(barrier, len(others) + trees - 1)
+    groups = nb // 2
+    group, place = s // 4, s % 4
+    near = (place // 2) * 2 + 1
+    group_order = [(group + g) % groups for g in (2, near, 4 - near, 0)]
 
     row = lax.broadcasted_iota(jnp.int32, w_send.shape[1:], 0)
 
@@ -153,27 +155,40 @@
                 x_send[j, other] = turned[other * part : other * part + quarter, :]
                 x_copy(j, other).start()
 
-    order = sorted(
-        (k + LAG[j], j, k) for k in range(half + 1) for j in range(len(OWNED))
-    )
-    started = False
-    for _, j, k in order:
-        if k < half:
+    def send_weights():
+        w_send[f] = weights(f)
+        w_recv[f] = weights(f)
+
+        @pl.loop(1, trees)
+        def _(r):
+            owner = (f + r) % trees
+            w_send[owner] = weights(owner)
+            w_copy(r, owner, f).start()
+
+    order = []
+    for j in range(len(OWNED)):
+        for k in range(half):
+            order.append((k + LAG[j], k > 0, j, 0, k))
+        for k in range(half - 1):
+            order.append((k + LAG[j], True, j, 1, k))
+        order.append((half + LAG[j], True, j, 2, half))
+    order.sort()
+    done = 1
+    multiply(group_order[0])
+    pl.semaphore_wait(barrier, trees + 1)
+    for slot, _, j, kind, k in order:
+        needed = 4 if k > 3 else 3 if k > 1 else 2 if (kind, k) != (0, 0) else 1
+        while done < needed:
+            multiply(group_order[done])
+            done += 1
+        if kind == 0:
             advance(k, j, *long_chain)
-        if k < half - 1:
+        elif kind == 1:
             advance(k, j, *short_chain)
-        if k == half:
+        else:
             finish(j)
-        if k == 1 and not started:
-            started = True
-            w_send[f] = weights(f)
-            w_recv[f] = weights(f)
-
-            @pl.loop(1, trees)
-            def _(r):
-                owner = (f + r) % trees
-                w_send[owner] = weights(owner)
-                w_copy(r, owner, f).start()
+        if (j, kind, k) == (len(OWNED) - 1, 1, 3):
+            send_weights()
 
     lane = lax.broadcasted_iota(jnp.int32, (quarter, block), 1)
     for j in range(SENT):
@@ -250,9 +265,10 @@
             lambda *refs: kernel(subs, trees, *refs),
             name="assemble",
             out_shape=jax.ShapeDtypeStruct((ANC_DEV, part, block), f32),
-            in_specs=[smem, smem, smem, vmem],
+            in_specs=[smem, smem, smem, pl.BlockSpec(memory_space=pl.ANY)],
             out_specs=vmem,
             scratch_shapes=[
+                pltpu.VMEM((nb, block, depth), jnp.bfloat16),
                 pltpu.VMEM((rows, depth), jnp.bfloat16),
                 pltpu.VMEM((nb, rows, block), f32),
                 pltpu.VMEM((half, owned, part, block), f32),
@@ -269,6 +285,7 @@
                 dma((SENT, 2)), dma((SENT, 2)),
                 dma((trees,)), dma((trees,)),
                 dma((trees,)), dma((trees,)),
+                dma(()),
             ],
             compiler_params=pltpu.CompilerParams(
                 collective_id=0, has_side_effects=True, vmem_limit_bytes=60 * 2**20

time: 71.3 us -> 69.8 us (0.979)
  Pallas kernels: 69.6 us -> 68 us
    pallas_call x1, Pallas kernels: 69.6 us -> 68 us  [per_device(): pl.pallas_call(lambda *refs: kernel(subs, trees, *refs), name='assemble',...]
where the time goes in v2:
time: 69.8 us; the launch traced here: 69.6 us
  Pallas kernels  68 us (97%)
  local copies, waits for them, and re-layouts  1.54 us (2%)
    pallas_call x1, Pallas kernels, per_device(): pl.pallas_call(lambda *refs: kernel(subs, trees, *refs), name='assemble',...  68 us
    unnamed x1, local copies, waits for them, and re-layouts  1.54 us

profile of v2, /device:TPU:1, one launch (start us, length us, event | category | flops | bytes accessed | tf_op | source)
XLA Modules:
  0.0 69.6 jit_solution(5500693590067228516)
XLA Ops:
  0.0 68.0 %assemble.1 = f32[3,64,128]{2,1,0:T(8,128)} custom-call(s32[8]{0:T(128)} %bitcast.8, s32[8,8]{1,0:T(8,128)} %bitcast.7, s32[8]{0:T(128)} %bitcast.9, bf16[8,128,2048]{2,1,0:T(8,128)(2,1)} %bitcast.5), custom_call_target="tpu_custom_call" | custom-call | tf_op jit(solution)/shard_map/assemble/pallas_call | solution.py:264
  68.0 1.5 %copy.6 = f32[1,3,64,128]{3,2,1,0:T(8,128)} copy(f32[1,3,64,128]{3,2,1,0:T(8,128)} %bitcast.6) | data formatting | bytes 196608

commit v3 on v2

--- a/solution.py
+++ b/solution.py
@@ -9,14 +9,15 @@
 ANC_DEV = 3
 OWNED = (5, 2, 1, 4, 0)
 SENT = 3
-LAG = (0, 0, 0, 0, 0)
+LAG = (0, 0, 0, 1, 1)
+STRIDE = 11
 
 
 def kernel(
     subs, trees,
     child_ref, pattern_ref, anc_ref, panel_hbm, out_ref,
     panel_ref, rows, gram, recv_l, recv_s, piece, x_send, x_recv, w_send, w_recv, t_send, t_recv,
-    l_out, l_in, s_out, s_in, x_out, x_in, w_out, w_in, t_out, t_in, panel_in,
+    l_out, l_in, s_out, s_in, x_out, x_in, w_out, w_in, t_out, t_in, panel_in, choice,
 ):
     nb = child_ref.shape[0]
     block = panel_hbm.shape[1]
@@ -47,10 +48,30 @@
             barrier, inc=1, device_id=(s, (f + r) % trees), device_id_type=MESH
         )
 
+    slots = w_send.shape
+    number = ANC_DEV * lax.broadcasted_iota(jnp.int32, slots, 0)
+    number += lax.broadcasted_iota(jnp.int32, slots, 1)
+    total = jnp.zeros(slots, jnp.float32)
+    for c in range(nb):
+        total += jnp.where(number == anc_ref[c], 1.0, 0.0)
+    w_send[...] = total
+    w_recv[f] = w_send[f]
+
+    @pl.loop(0, trees)
+    def _(owner):
+        index = jnp.int32(nb)
+        for c in range(nb):
+            first = anc_ref[c] - ANC_DEV * owner
+            index = jnp.where((first >= 0) & (first < ANC_DEV), c, index)
+        choice[owner] = index
+
+    piece[nb] = jnp.zeros(piece.shape[1:], jnp.float32)
+
     load.wait()
 
-    @pl.loop(0, nb)
-    def _(to):
+    @pl.loop(0, nb + 2)
+    def _(place):
+        to = place % nb
         source = jnp.int32(0)
         for i in range(nb):
             source = jnp.where(child_ref[i] == to, i, source)
@@ -58,30 +79,22 @@
         for i in range(nb):
             keep = jnp.where(child_ref[i] == to, pattern_ref[i, i], keep)
         chunk = panel_ref[source]
-        rows[pl.ds(pl.multiple_of(to * block, block), block), :] = chunk * keep.astype(
+        rows[pl.ds(pl.multiple_of(place * block, block), block), :] = chunk * keep.astype(
             jnp.float32
         ).astype(jnp.bfloat16)
 
-    def multiply(u):
-        at = pl.ds(pl.multiple_of(u * 2 * block, 2 * block), 2 * block)
+    def multiply(w, q):
+        first = (s + half - 1 + 4 * w) % subs
         product = lax.dot_general(
-            rows[at, :], rows[...], (((1,), (1,)), ((), ())), preferred_element_type=jnp.float32
-        )
-        for n in range(nb):
-            gram[n, at, :] = product[:, n * block : (n + 1) * block]
-
-    groups = nb // 2
-    group, place = s // 4, s % 4
-    near = (place // 2) * 2 + 1
-    group_order = [(group + g) % groups for g in (2, near, 4 - near, 0)]
-
-    row = lax.broadcasted_iota(jnp.int32, w_send.shape[1:], 0)
-
-    def weights(owner):
-        total = jnp.zeros(row.shape, jnp.float32)
-        for c in range(nb):
-            total += jnp.where(row == anc_ref[c] - ANC_DEV * owner, 1.0, 0.0)
-        return total
+            rows[pl.ds(pl.multiple_of(first * part, part), 4 * part), :],
+            rows[q * 2 * block : (q + 1) * 2 * block, :],
+            (((1,), (1,)), ((), ())),
+            preferred_element_type=jnp.float32,
+        )
+        for h in (0, 1):
+            gram[2 * q + h, 4 * w * part : 4 * (w + 1) * part, :] = product[
+                :, h * block : (h + 1) * block
+            ]
 
     def w_copy(r, owner, source):
         return pltpu.make_async_remote_copy(
@@ -97,18 +110,15 @@
             device_id=(s, owner), device_id_type=MESH,
         )
 
-    def own(target, j):
+    def own(offset, j):
+        at = (offset + 2 * subs - half + 1) % subs
         return gram.at[
-            block_row_of(target, j), pl.ds(pl.multiple_of(target * part, part), part), :
+            (z(offset) // 2 + OWNED[j]) % nb, pl.ds(pl.multiple_of(at * part, part), part), :
         ]
 
-    def block_row_of(target, j):
-        return (target // 2 + OWNED[j]) % nb
-
     def chain(k, j, buffers, outs, ins, direction, steps):
-        target = z(direction * (steps - k))
         if k == 0:
-            source = own(target, j)
+            source = own(direction * steps, j)
         else:
             source = buffers.at[k - 1, j]
         return pltpu.make_async_remote_copy(
@@ -120,7 +130,7 @@
     def advance(k, j, buffers, outs, ins, direction, steps):
         if k > 0:
             chain(k - 1, j, buffers, outs, ins, direction, steps).wait_recv()
-            buffers[k - 1, j] = buffers[k - 1, j] + own(z(direction * (steps - k)), j)[...]
+            buffers[k - 1, j] = buffers[k - 1, j] + own(direction * (steps - k), j)[...]
         chain(k, j, buffers, outs, ins, direction, steps).start()
 
     long_chain = (recv_l, l_out, l_in, sigma, half)
@@ -146,7 +156,7 @@
     def finish(j):
         chain(half - 1, j, *long_chain).wait_recv()
         chain(half - 2, j, *short_chain).wait_recv()
-        tile = own(z(0), j)[...] + (recv_l[half - 1, j] + recv_s[half - 2, j])
+        tile = own(0, j)[...] + (recv_l[half - 1, j] + recv_s[half - 2, j])
         piece[block_row(OWNED[j])] = tile
         if j < SENT:
             stacked = jnp.concatenate([tile, pltpu.roll(tile, block - quarter, 1)], axis=0)
@@ -155,40 +165,44 @@
                 x_send[j, other] = turned[other * part : other * part + quarter, :]
                 x_copy(j, other).start()
 
-    def send_weights():
-        w_send[f] = weights(f)
-        w_recv[f] = weights(f)
-
-        @pl.loop(1, trees)
+    def send_weights(low, high):
+        @pl.loop(low, high)
         def _(r):
             owner = (f + r) % trees
-            w_send[owner] = weights(owner)
             w_copy(r, owner, f).start()
+
+    beside = {}
+    for q in range(nb // 2):
+        beside[1, q] = [(multiply, 1, q)]
+        beside[2 + q // 2, 1 + 2 * (q % 2)] = [(multiply, 2, q)]
+        beside[4 + q // 2, 1 + 2 * (q % 2)] = [
+            (send_weights, max(1, trees * q // 4), trees * (q + 1) // 4)
+        ]
 
     order = []
     for j in range(len(OWNED)):
         for k in range(half):
-            order.append((k + LAG[j], k > 0, j, 0, k))
+            order.append((k + LAG[j], j, 0, k))
         for k in range(half - 1):
-            order.append((k + LAG[j], True, j, 1, k))
-        order.append((half + LAG[j], True, j, 2, half))
+            order.append((k + LAG[j], j, 1, k))
+        order.append((half + LAG[j], j, 2, half))
     order.sort()
-    done = 1
-    multiply(group_order[0])
+    for q in range(nb // 2):
+        multiply(0, q)
     pl.semaphore_wait(barrier, trees + 1)
-    for slot, _, j, kind, k in order:
-        needed = 4 if k > 3 else 3 if k > 1 else 2 if (kind, k) != (0, 0) else 1
-        while done < needed:
-            multiply(group_order[done])
-            done += 1
+    for at, (slot, j, kind, k) in enumerate(order):
+        if slot == 1 and order[at - 1][0] == 0:
+            for q in range(nb // 2):
+                multiply(3, q)
         if kind == 0:
             advance(k, j, *long_chain)
         elif kind == 1:
             advance(k, j, *short_chain)
         else:
             finish(j)
-        if (j, kind, k) == (len(OWNED) - 1, 1, 3):
-            send_weights()
+        if at + 1 == len(order) or order[at + 1][:2] != (slot, j):
+            for work, *given in beside.pop((slot, j), []):
+                work(*given)
 
     lane = lax.broadcasted_iota(jnp.int32, (quarter, block), 1)
     for j in range(SENT):
@@ -199,19 +213,10 @@
         n = block_row(-OWNED[j])
         piece[n, :quarter, :] = jnp.where(lane < part, low, pltpu.roll(high, part, 1))
         piece[n, quarter:, :] = jnp.where(lane < part, pltpu.roll(low, part, 1), high)
-    piece[nb] = jnp.zeros(piece.shape[1:], jnp.float32)
-
-    def chosen(owner):
-        index = jnp.int32(nb)
-        for c in range(nb):
-            first = anc_ref[c] - ANC_DEV * owner
-            index = jnp.where((first >= 0) & (first < ANC_DEV), c, index)
-        return piece[index]
-
     @pl.loop(1, trees)
     def _(r):
-        owner = (f + r) % trees
-        t_send[owner] = chosen(owner)
+        owner = (f + STRIDE * r) % trees
+        t_send[owner] = piece[choice[owner]]
         t_copy(r, owner, f).start()
 
     def added(source, tile, totals):
@@ -219,13 +224,17 @@
         return tuple(totals[a] + weight[a : a + 1, :] * tile for a in range(ANC_DEV))
 
     zero = jnp.zeros(piece.shape[1:], jnp.float32)
-    totals = added(f, chosen(f), (zero,) * ANC_DEV)
+    totals = added(f, piece[choice[f]], (zero,) * ANC_DEV)
 
     def gather(r, totals):
+        source = (f + STRIDE * (trees - r)) % trees
+        t_copy(r, source, source).wait_recv()
+        return added(source, t_recv[source], totals)
+
+    @pl.loop(1, trees)
+    def _(r):
         source = (f + trees - r) % trees
         w_copy(r, source, source).wait_recv()
-        t_copy(r, source, source).wait_recv()
-        return added(source, t_recv[source], totals)
 
     totals = lax.fori_loop(1, trees, gather, totals)
     for a in range(ANC_DEV):
@@ -242,9 +251,8 @@
 
     @pl.loop(1, trees)
     def _(r):
-        owner = (f + r) % trees
-        w_copy(r, owner, f).wait_send()
-        t_copy(r, owner, f).wait_send()
+        w_copy(r, (f + r) % trees, f).wait_send()
+        t_copy(r, (f + STRIDE * r) % trees, f).wait_send()
 
 
 def solution(mesh):
@@ -269,7 +277,7 @@
             out_specs=vmem,
             scratch_shapes=[
                 pltpu.VMEM((nb, block, depth), jnp.bfloat16),
-                pltpu.VMEM((rows, depth), jnp.bfloat16),
+                pltpu.VMEM((rows + 2 * block, depth), jnp.bfloat16),
                 pltpu.VMEM((nb, rows, block), f32),
                 pltpu.VMEM((half, owned, part, block), f32),
                 pltpu.VMEM((half - 1, owned, part, block), f32),
@@ -286,6 +294,7 @@
                 dma((trees,)), dma((trees,)),
                 dma((trees,)), dma((trees,)),
                 dma(()),
+                pltpu.SMEM((trees,), jnp.int32),
             ],
             compiler_params=pltpu.CompilerParams(
                 collective_id=0, has_side_effects=True, vmem_limit_bytes=60 * 2**20

time: 69.8 us -> 67.9 us (0.973)
  Pallas kernels: 68 us -> 66.2 us
    pallas_call x1, Pallas kernels: 68 us -> 66.2 us  [per_device(): pl.pallas_call(lambda *refs: kernel(subs, trees, *refs), name='assemble',...]
where the time goes in v3:
time: 67.9 us; the launch traced here: 67.7 us
  Pallas kernels  66.2 us (97%)
  local copies, waits for them, and re-layouts  1.54 us (2%)
    pallas_call x1, Pallas kernels, per_device(): pl.pallas_call(lambda *refs: kernel(subs, trees, *refs), name='assemble',...  66.2 us
    unnamed x1, local copies, waits for them, and re-layouts  1.54 us

profile of v3, /device:TPU:1, one launch (start us, length us, event | category | flops | bytes accessed | tf_op | source)
XLA Modules:
  0.0 67.7 jit_solution(16498923205393698112)
XLA Ops:
  0.0 66.2 %assemble.1 = f32[3,64,128]{2,1,0:T(8,128)} custom-call(s32[8]{0:T(128)} %bitcast.8, s32[8,8]{1,0:T(8,128)} %bitcast.7, s32[8]{0:T(128)} %bitcast.9, bf16[8,128,2048]{2,1,0:T(8,128)(2,1)} %bitcast.5), custom_call_target="tpu_custom_call" | custom-call | tf_op jit(solution)/shard_map/assemble/pallas_call | solution.py:272
  66.2 1.5 %copy.6 = f32[1,3,64,128]{3,2,1,0:T(8,128)} copy(f32[1,3,64,128]{3,2,1,0:T(8,128)} %bitcast.6) | data formatting | bytes 196608

commit v4 on v3

--- a/solution.py
+++ b/solution.py
@@ -272,7 +272,7 @@
         out = pl.pallas_call(
             lambda *refs: kernel(subs, trees, *refs),
             name="assemble",
-            out_shape=jax.ShapeDtypeStruct((ANC_DEV, part, block), f32),
+            out_shape=pltpu.VMEM((ANC_DEV, part, block), f32),
             in_specs=[smem, smem, smem, pl.BlockSpec(memory_space=pl.ANY)],
             out_specs=vmem,
             scratch_shapes=[

time: 67.9 us -> 66.4 us (0.978)
  local copies, waits for them, and re-layouts: 1.54 us -> 0.64 us
  Pallas kernels: 66.2 us -> 65.5 us
    unnamed x1, local copies, waits for them, and re-layouts: 1.54 us -> 0.64 us
where the time goes in v4:
time: 66.4 us; the launch traced here: 66.2 us
  Pallas kernels  65.5 us (99%)
    pallas_call x1, Pallas kernels, per_device(): pl.pallas_call(lambda *refs: kernel(subs, trees, *refs), name='assemble',...  65.5 us

profile of v4, /device:TPU:1, one launch (start us, length us, event | category | flops | bytes accessed | tf_op | source)
XLA Modules:
  0.0 66.2 jit_solution(10767342679528355659)
XLA Ops:
  0.0 65.5 %assemble.1 = f32[3,64,128]{2,1,0:T(8,128)S(1)} custom-call(s32[8]{0:T(128)} %bitcast.8, s32[8,8]{1,0:T(8,128)} %bitcast.7, s32[8]{0:T(128)} %bitcast.9, bf16[8,128,2048]{2,1,0:T(8,128)(2,1)} %bitcast.6), custom_call_target="tpu_custom_call" | custom-call | tf_op jit(solution)/shard_map/assemble/pallas_call | solution.py:272
  65.5 0.6 copy.6

commit v5 on v4

--- a/solution.py
+++ b/solution.py
@@ -7,9 +7,9 @@
 
 MESH = pl.DeviceIdType.MESH
 ANC_DEV = 3
-OWNED = (5, 2, 1, 4, 0)
-SENT = 3
-LAG = (0, 0, 0, 1, 1)
+OWNED = (4, 5, 2, 1, 0)
+SENT = (1, 2, 3)
+LAG = (0, 0, 0, 0, 0)
 STRIDE = 11
 
 
@@ -18,6 +18,7 @@
     child_ref, pattern_ref, anc_ref, panel_hbm, out_ref,
     panel_ref, rows, gram, recv_l, recv_s, piece, x_send, x_recv, w_send, w_recv, t_send, t_recv,
     l_out, l_in, s_out, s_in, x_out, x_in, w_out, w_in, t_out, t_in, panel_in, choice,
+    first_l, first_s, y_own, y_send, y_recv, y_out, y_in,
 ):
     nb = child_ref.shape[0]
     block = panel_hbm.shape[1]
@@ -116,53 +117,92 @@
             (z(offset) // 2 + OWNED[j]) % nb, pl.ds(pl.multiple_of(at * part, part), part), :
         ]
 
-    def chain(k, j, buffers, outs, ins, direction, steps):
-        if k == 0:
+    quarter = part // 2
+    lane = lax.broadcasted_iota(jnp.int32, (quarter, block), 1)
+
+    def half_of(offset):
+        row, its_side = z(offset) // 2, z(offset) % 2
+        upper = row // (nb // 2)
+        return its_side * (1 - upper) + (1 - its_side) * upper
+
+    def turn(value):
+        return pltpu.roll(value, part, 1)
+
+    def mine(offset, j):
+        tile = own(offset, j)[...]
+        if j > 0:
+            return tile
+        which = jnp.full(tile.shape, half_of(offset), jnp.int32)
+        tile = jnp.where(which == 0, tile, turn(tile))
+        return jnp.where(lane < part, tile[:quarter], turn(tile[quarter:]))
+
+    def at_tile(j):
+        return pl.ds(0, quarter) if j == 0 else pl.ds(quarter + part * (j - 1), part)
+
+    def chain(k, j, first, buffers, outs, ins, direction, steps):
+        if k > 0:
+            source = buffers.at[k - 1, at_tile(j)]
+        elif j > 0:
             source = own(direction * steps, j)
         else:
-            source = buffers.at[k - 1, j]
-        return pltpu.make_async_remote_copy(
-            src_ref=source, dst_ref=buffers.at[k, j],
+            source = first
+        return pltpu.make_async_remote_copy(
+            src_ref=source, dst_ref=buffers.at[k, at_tile(j)],
             send_sem=outs.at[k, j], recv_sem=ins.at[k, j],
             device_id=(z(direction), f), device_id_type=MESH,
         )
 
-    def advance(k, j, buffers, outs, ins, direction, steps):
+    def advance(k, j, first, buffers, outs, ins, direction, steps):
         if k > 0:
-            chain(k - 1, j, buffers, outs, ins, direction, steps).wait_recv()
-            buffers[k - 1, j] = buffers[k - 1, j] + own(direction * (steps - k), j)[...]
-        chain(k, j, buffers, outs, ins, direction, steps).start()
-
-    long_chain = (recv_l, l_out, l_in, sigma, half)
-    short_chain = (recv_s, s_out, s_in, -sigma, half - 1)
+            term = mine(direction * (steps - k), j)
+            chain(k - 1, j, first, buffers, outs, ins, direction, steps).wait_recv()
+            buffers[k - 1, at_tile(j)] = buffers[k - 1, at_tile(j)] + term
+        elif j == 0:
+            first[...] = mine(direction * steps, j)
+        chain(k, j, first, buffers, outs, ins, direction, steps).start()
+
+    long_chain = (first_l, recv_l, l_out, l_in, sigma, half)
+    short_chain = (first_s, recv_s, s_out, s_in, -sigma, half - 1)
+    my_half = half_of(0)
+    y_copy = pltpu.make_async_remote_copy(
+        src_ref=y_send, dst_ref=y_recv, send_sem=y_out, recv_sem=y_in,
+        device_id=(2 * block_row(nb // 2) + my_half, f), device_id_type=MESH,
+    )
 
     def x_copy(j, other):
         n = block_row(OWNED[j])
         return pltpu.make_async_remote_copy(
-            src_ref=x_send.at[j, other], dst_ref=x_recv.at[j, side],
-            send_sem=x_out.at[j, other], recv_sem=x_in.at[j, side],
+            src_ref=x_send.at[j - 1, other], dst_ref=x_recv.at[j - 1, side],
+            send_sem=x_out.at[j - 1, other], recv_sem=x_in.at[j - 1, side],
             device_id=(2 * n + other, f), device_id_type=MESH,
         )
 
     def x_arrival(j, other):
         return pltpu.make_async_remote_copy(
-            src_ref=x_send.at[j, other], dst_ref=x_recv.at[j, other],
-            send_sem=x_out.at[j, other], recv_sem=x_in.at[j, other],
+            src_ref=x_send.at[j - 1, other], dst_ref=x_recv.at[j - 1, other],
+            send_sem=x_out.at[j - 1, other], recv_sem=x_in.at[j - 1, other],
             device_id=(2 * block_row(OWNED[j]) + other, f), device_id_type=MESH,
         )
 
-    quarter = part // 2
-
     def finish(j):
+        term = mine(0, j)
         chain(half - 1, j, *long_chain).wait_recv()
         chain(half - 2, j, *short_chain).wait_recv()
-        tile = own(0, j)[...] + (recv_l[half - 1, j] + recv_s[half - 2, j])
-        piece[block_row(OWNED[j])] = tile
-        if j < SENT:
+        tile = term + (recv_l[half - 1, at_tile(j)] + recv_s[half - 2, at_tile(j)])
+        if j == 0:
+            y_own[...] = tile
+            tile = jnp.concatenate([tile, turn(tile)], axis=0)
+        else:
+            piece[block_row(OWNED[j])] = tile
+        if j == 0 or j in SENT:
             stacked = jnp.concatenate([tile, pltpu.roll(tile, block - quarter, 1)], axis=0)
             turned = stacked.T
+        if j == 0:
+            y_send[...] = turned[:quarter, :]
+            y_copy.start()
+        elif j in SENT:
             for other in (0, 1):
-                x_send[j, other] = turned[other * part : other * part + quarter, :]
+                x_send[j - 1, other] = turned[other * part : other * part + quarter, :]
                 x_copy(j, other).start()
 
     def send_weights(low, high):
@@ -204,15 +244,22 @@
             for work, *given in beside.pop((slot, j), []):
                 work(*given)
 
-    lane = lax.broadcasted_iota(jnp.int32, (quarter, block), 1)
-    for j in range(SENT):
+    def put(n, low, high):
+        piece[n, :quarter, :] = jnp.where(lane < part, low, turn(high))
+        piece[n, quarter:, :] = jnp.where(lane < part, turn(low), high)
+
+    for j in reversed(SENT):
         for other in (0, 1):
             x_arrival(j, other).wait_recv()
-        low = x_recv[j, 0]
-        high = x_recv[j, 1]
-        n = block_row(-OWNED[j])
-        piece[n, :quarter, :] = jnp.where(lane < part, low, pltpu.roll(high, part, 1))
-        piece[n, quarter:, :] = jnp.where(lane < part, pltpu.roll(low, part, 1), high)
+        put(block_row(-OWNED[j]), x_recv[j - 1, 0], x_recv[j - 1, 1])
+    y_copy.wait_recv()
+    which = jnp.full(lane.shape, my_half, jnp.int32)
+    put(
+        block_row(nb // 2),
+        jnp.where(which == 0, y_own[...], y_recv[...]),
+        jnp.where(which == 0, y_recv[...], y_own[...]),
+    )
+
     @pl.loop(1, trees)
     def _(r):
         owner = (f + STRIDE * r) % trees
@@ -245,7 +292,8 @@
             chain(k, j, *long_chain).wait_send()
         for k in range(half - 1):
             chain(k, j, *short_chain).wait_send()
-    for j in range(SENT):
+    y_copy.wait_send()
+    for j in SENT:
         for other in (0, 1):
             x_copy(j, other).wait_send()
 
@@ -279,22 +327,28 @@
                 pltpu.VMEM((nb, block, depth), jnp.bfloat16),
                 pltpu.VMEM((rows + 2 * block, depth), jnp.bfloat16),
                 pltpu.VMEM((nb, rows, block), f32),
-                pltpu.VMEM((half, owned, part, block), f32),
-                pltpu.VMEM((half - 1, owned, part, block), f32),
+                pltpu.VMEM((half, part * owned - part // 2, block), f32),
+                pltpu.VMEM((half - 1, part * owned - part // 2, block), f32),
                 pltpu.VMEM((nb + 1, part, block), f32),
-                pltpu.VMEM((SENT, 2, part // 2, block), f32),
-                pltpu.VMEM((SENT, 2, part // 2, block), f32),
+                pltpu.VMEM((len(SENT), 2, part // 2, block), f32),
+                pltpu.VMEM((len(SENT), 2, part // 2, block), f32),
                 pltpu.VMEM((trees, 8, block), f32),
                 pltpu.VMEM((trees, 8, block), f32),
                 pltpu.VMEM((trees, part, block), f32),
                 pltpu.VMEM((trees, part, block), f32),
                 dma((half, owned)), dma((half, owned)),
                 dma((half - 1, owned)), dma((half - 1, owned)),
-                dma((SENT, 2)), dma((SENT, 2)),
+                dma((len(SENT), 2)), dma((len(SENT), 2)),
                 dma((trees,)), dma((trees,)),
                 dma((trees,)), dma((trees,)),
                 dma(()),
                 pltpu.SMEM((trees,), jnp.int32),
+                pltpu.VMEM((part // 2, block), f32),
+                pltpu.VMEM((part // 2, block), f32),
+                pltpu.VMEM((part // 2, block), f32),
+                pltpu.VMEM((part // 2, block), f32),
+                pltpu.VMEM((part // 2, block), f32),
+                dma(()), dma(()),
             ],
             compiler_params=pltpu.CompilerParams(
                 collective_id=0, has_side_effects=True, vmem_limit_bytes=60 * 2**20

time: 66.4 us -> 66 us (level)
  no operation moved by 1% of the time
where the time goes in v5:
time: 66 us; the launch traced here: 65.9 us
  Pallas kernels  65.2 us (99%)
    pallas_call x1, Pallas kernels, per_device(): pl.pallas_call(lambda *refs: kernel(subs, trees, *refs), name='assemble',...  65.2 us

profile of v5, /device:TPU:1, one launch (start us, length us, event | category | flops | bytes accessed | tf_op | source)
XLA Modules:
  0.0 65.9 jit_solution(7141111114283366940)
XLA Ops:
  0.0 65.2 %assemble.1 = f32[3,64,128]{2,1,0:T(8,128)S(1)} custom-call(s32[8]{0:T(128)} %bitcast.8, s32[8,8]{1,0:T(8,128)} %bitcast.7, s32[8]{0:T(128)} %bitcast.9, bf16[8,128,2048]{2,1,0:T(8,128)(2,1)} %bitcast.6), custom_call_target="tpu_custom_call" | custom-call | tf_op jit(solution)/shard_map/assemble/pallas_call | solution.py:320
  65.2 0.6 copy.6

commit v6 on v5

--- a/solution.py
+++ b/solution.py
@@ -10,7 +10,6 @@
 OWNED = (4, 5, 2, 1, 0)
 SENT = (1, 2, 3)
 LAG = (0, 0, 0, 0, 0)
-STRIDE = 11
 
 
 def kernel(
@@ -260,9 +259,22 @@
         jnp.where(which == 0, y_recv[...], y_own[...]),
     )
 
-    @pl.loop(1, trees)
-    def _(r):
-        owner = (f + STRIDE * r) % trees
+    across = (trees // 8, 4, 2)
+    steps = [(a, b, c) for a in range(across[0]) for b in range(4) for c in range(2)][1:]
+
+    def hops(step):
+        return sum(min(d, n - d) for d, n in zip(step[:2], across[:2]))
+
+    steps.sort(key=hops, reverse=True)
+
+    def moved(step, sign):
+        y, x, core = f // 8, f // 2 % 4, f % 2
+        y = (y + sign * step[0] + across[0]) % across[0]
+        x = (x + sign * step[1] + 4) % 4
+        return y * 8 + x * 2 + (core + step[2]) % 2
+
+    for r, step in enumerate(steps):
+        owner = moved(step, 1)
         t_send[owner] = piece[choice[owner]]
         t_copy(r, owner, f).start()
 
@@ -272,18 +284,16 @@
 
     zero = jnp.zeros(piece.shape[1:], jnp.float32)
     totals = added(f, piece[choice[f]], (zero,) * ANC_DEV)
-
-    def gather(r, totals):
-        source = (f + STRIDE * (trees - r)) % trees
-        t_copy(r, source, source).wait_recv()
-        return added(source, t_recv[source], totals)
 
     @pl.loop(1, trees)
     def _(r):
         source = (f + trees - r) % trees
         w_copy(r, source, source).wait_recv()
 
-    totals = lax.fori_loop(1, trees, gather, totals)
+    for r, step in enumerate(steps):
+        source = moved(step, -1)
+        t_copy(r, source, source).wait_recv()
+        totals = added(source, t_recv[source], totals)
     for a in range(ANC_DEV):
         out_ref[a] = totals[a]
 
@@ -300,7 +310,9 @@
     @pl.loop(1, trees)
     def _(r):
         w_copy(r, (f + r) % trees, f).wait_send()
-        t_copy(r, (f + STRIDE * r) % trees, f).wait_send()
+
+    for r, step in enumerate(steps):
+        t_copy(r, moved(step, 1), f).wait_send()
 
 
 def solution(mesh):

time: 66 us -> 66.2 us (level)
  no operation moved by 1% of the time
where the time goes in v6:
time: 66.2 us; the launch traced here: 66 us
  Pallas kernels  65.3 us (99%)
    pallas_call x1, Pallas kernels, per_device(): pl.pallas_call(lambda *refs: kernel(subs, trees, *refs), name='assemble',...  65.3 us

profile of v6, /device:TPU:1, one launch (start us, length us, event | category | flops | bytes accessed | tf_op | source)
XLA Modules:
  0.0 66.0 jit_solution(8294994534828401037)
XLA Ops:
  0.0 65.3 %assemble.1 = f32[3,64,128]{2,1,0:T(8,128)S(1)} custom-call(s32[8]{0:T(128)} %bitcast.8, s32[8,8]{1,0:T(8,128)} %bitcast.7, s32[8]{0:T(128)} %bitcast.9, bf16[8,128,2048]{2,1,0:T(8,128)(2,1)} %bitcast.6), custom_call_target="tpu_custom_call" | custom-call | tf_op jit(solution)/shard_map/assemble/pallas_call | solution.py:332
  65.4 0.6 copy.6
